TPU v7x, 512 devices: a whole 4x4x16 slice. The times are simulated.
512 devices in a mesh: tm: 64 (over y, z), head: 8 (over x, core).
Axes of the slice: x: 4, y: 4, z: 16, core: 2. Of those that a mesh axis runs over, the one named last changes fastest.
Arguments:
- frames: bfloat16 [16384, 1024], P('tm'), may hold values from -6 to 6
- x_weight: bfloat16 [1024, 2048], P('tm', 'head'), may hold values from -0.1875 to 0.1875
- z_weight: bfloat16 [1024, 2048], P('tm', 'head'), may hold values from -0.1875 to 0.1875
- bc_weight: bfloat16 [1024, 256], P('tm'), may hold values from -0.1875 to 0.1875
- log_decay: float32 [32, 16384], P('head', 'tm'), may hold values from -0.9 to 0
- norm_gain: float32 [2048], P('head'), may hold values from 0.1 to 1.9
- conv_weight: float32 [31, 2048], P(None, 'head'), may hold values from -1 to 1
- out_weight: bfloat16 [2048, 1024], P('head', 'tm'), may hold values from -0.125 to 0.125
- record_lengths: int32 [8], replicated, may hold values from 1 to 12288, 16384 in all
Outputs:
- mixed: bfloat16 [16384, 1024], P('tm', 'head')
Inputs may be any that keep to these rules, and one draw needn't show every extreme that they name: `record_lengths`: 8 recording lengths that sum to 16384; the longest has exactly 12288 frames.
All inputs are finite; a program needn't handle non-finite values.
Results may differ from a plain program's by a relative error of at most 0.02.
Values may be sent and summed in bfloat16 or wider, within the bound.
A program may use at most 64 MiB of HBM per device.

v0:
```python
import jax
import jax.numpy as jnp
from jax import lax
from jax.sharding import PartitionSpec as P

SPAN = 128
highest = lax.Precision.HIGHEST


def extended_2(array, sides, width):
    for axis, dim in sides:
        peers, length = (lax.axis_size(axis), array.shape[dim])
        up = [(i, (i + 1) % peers) for i in range(peers - 1)]
        down = [(j, i) for i, j in up]
        last = lax.slice_in_dim(array, length - width, length, axis=dim)
        leading = lax.slice_in_dim(array, 0, width, axis=dim)
        before = lax.ppermute(last, axis, up)
        after = lax.ppermute(leading, axis, down)
        array = jnp.concatenate([before, array, after], axis=dim)
    return array


def segment_ids(record_lengths, positions):
    record_ends = jnp.cumsum(record_lengths)
    return jnp.sum((record_ends[None, :] <= positions[:, None]).astype(jnp.int32), axis=1)


def span_step(state, inputs):
    x_block, b_block, c_block, log_block, seg_block, seg_before = inputs
    length = seg_block.shape[0]
    cumul = jnp.cumsum(log_block, axis=1)
    lower = jnp.arange(length)[:, None] >= jnp.arange(length)[None, :]
    joined = (seg_block[:, None] == seg_block[None, :]) & lower
    spread = cumul[:, :, None] - cumul[:, None, :]
    mixing = jnp.exp(jnp.where(joined[None], spread, -jnp.inf))
    scores = jnp.dot(c_block, b_block.T, preferred_element_type=jnp.float32)
    x_float = x_block.astype(jnp.float32)
    inner = jnp.einsum("hts,shp->thp", mixing * scores[None], x_float, precision=highest)
    carried = jnp.exp(cumul) * (seg_block == seg_before).astype(jnp.float32)[None, :]
    c_float = c_block.astype(jnp.float32)
    outer = jnp.einsum("tn,hnp->thp", c_float, state, precision=highest) * carried.T[:, :, None]
    tail = (
        jnp.exp(cumul[:, -1:] - cumul) * (seg_block == seg_block[-1]).astype(jnp.float32)[None, :]
    )
    weighted = tail[:, :, None] * b_block.astype(jnp.float32)[None, :, :]
    state_next = carried[:, -1][:, None, None] * state + jnp.einsum(
        "hsn,shp->hnp", weighted, x_float, precision=highest
    )
    return (state_next, inner + outer)


def run_spans(x_rows, b_rows, c_rows, log_rows, seg_rows, seg_first, state):
    count = x_rows.shape[0] // SPAN
    heads_here = log_rows.shape[0]
    x_blocks = x_rows.reshape(count, SPAN, heads_here, -1)
    b_blocks = b_rows.reshape(count, SPAN, -1)
    c_blocks = c_rows.reshape(count, SPAN, -1)
    log_blocks = log_rows.reshape(heads_here, count, SPAN).transpose(1, 0, 2)
    seg_blocks = seg_rows.reshape(count, SPAN)
    seg_befores = jnp.concatenate([jnp.reshape(seg_first, (1,)), seg_blocks[:-1, -1]])
    state, outputs = lax.scan(
        span_step, state, (x_blocks, b_blocks, c_blocks, log_blocks, seg_blocks, seg_befores)
    )
    return (state, outputs.reshape(count * SPAN, heads_here, -1))


def gate_rows(ssd_out, z_rows, norm_gain):
    square_mean = jnp.mean(ssd_out * ssd_out, axis=-1, keepdims=True)
    normed = (ssd_out * lax.rsqrt(square_mean + 1e-05)).reshape(ssd_out.shape[0], -1)
    z_float = z_rows.astype(jnp.float32)
    return (normed * norm_gain[None, :] * z_float * jax.nn.sigmoid(z_float)).astype(jnp.bfloat16)


def conv_rows(extended, seg_extended, seg_rows, conv_weight):
    frame_count = seg_rows.shape[0]
    summed = jnp.zeros((frame_count, extended.shape[1]), jnp.float32)
    for offset in range(conv_weight.shape[0]):
        same = (seg_extended[offset : offset + frame_count] == seg_rows).astype(jnp.float32)
        summed = (
            summed
            + conv_weight[offset][None, :]
            * extended[offset : offset + frame_count].astype(jnp.float32)
            * same[:, None]
        )
    return (summed * jax.nn.sigmoid(summed)).astype(jnp.bfloat16)


def local(
    frames,
    x_weight,
    z_weight,
    bc_weight,
    log_decay,
    norm_gain,
    conv_weight,
    out_weight,
    record_lengths,
):
    frame_count = frames.shape[0]
    state_width = bc_weight.shape[1] // 2
    pieces = (
        lax.all_gather(x_weight, "tm", axis=0, tiled=True),
        lax.all_gather(z_weight, "tm", axis=0, tiled=True),
        lax.all_gather(bc_weight, "tm", axis=0, tiled=True),
    )
    x_sum, z_sum, bc_sum = tuple(
        (jnp.dot(frames, weight_rows, preferred_element_type=jnp.float32) for weight_rows in pieces)
    )
    bc_rows = bc_sum.astype(jnp.bfloat16)
    x_rows = x_sum.astype(jnp.bfloat16)
    z_rows = z_sum.astype(jnp.bfloat16)
    dev_start = lax.axis_index("tm") * frame_count
    positions = dev_start + jnp.arange(frame_count, dtype=jnp.int32)
    seg_rows = segment_ids(record_lengths, positions)
    seg_before_dev = segment_ids(record_lengths, jnp.reshape(dev_start - 1, (1,)))[0]
    seg_first = jnp.where(dev_start == 0, -1, seg_before_dev)
    heads_here = log_decay.shape[0]
    head_size = x_weight.shape[1] // heads_here
    empty_state = jnp.zeros((heads_here, state_width, head_size), jnp.float32)
    local_state, local_out = run_spans(
        x_rows,
        bc_rows[:, :state_width],
        bc_rows[:, state_width:],
        log_decay,
        seg_rows,
        seg_first,
        empty_state,
    )
    same_first = (seg_rows == seg_first).astype(jnp.float32)
    through = jnp.exp(jnp.sum(log_decay, axis=1)) * same_first[-1]
    all_keep, all_summaries = (
        lax.all_gather(through[None], "tm", axis=0, tiled=True),
        lax.all_gather(local_state[None], "tm", axis=0, tiled=True),
    )
    dev_index = lax.axis_index("tm")

    def absorb(position, carry_state):
        updated = all_keep[position][:, None, None] * carry_state + all_summaries[position]
        return jnp.where(position < dev_index, updated, carry_state)

    entry_state = lax.fori_loop(0, all_keep.shape[0], absorb, empty_state)
    growth = jnp.exp(jnp.cumsum(log_decay, axis=1)) * same_first[None, :]
    carried = (
        jnp.einsum(
            "tn,hnp->thp",
            bc_rows[:, state_width:].astype(jnp.float32),
            entry_state,
            precision=highest,
        )
        * growth.T[:, :, None]
    )
    ssd_out = local_out + carried
    gated = gate_rows(ssd_out, z_rows, norm_gain)
    half_width = (conv_weight.shape[0] - 1) // 2
    extended = extended_2(gated, (("tm", 0),), half_width)
    seg_extended = segment_ids(
        record_lengths,
        dev_start - half_width + jnp.arange(frame_count + 2 * half_width, dtype=jnp.int32),
    )
    act_rows = conv_rows(extended, seg_extended, seg_rows, conv_weight)
    partial_terms = jnp.dot(
        act_rows,
        lax.all_gather(out_weight, "tm", axis=1, tiled=True),
        preferred_element_type=jnp.float32,
    )
    return lax.psum_scatter(
        partial_terms.astype(jnp.bfloat16), "head", scatter_dimension=1, tiled=True
    )


def solution(mesh):
    in_specs = (
        P("tm", None),
        P("tm", "head"),
        P("tm", "head"),
        P("tm", None),
        P("head", "tm"),
        P("head"),
        P(None, "head"),
        P("head", "tm"),
        P(),
    )
    out_specs = P("tm", "head")
    return jax.shard_map(local, mesh=mesh, in_specs=in_specs, out_specs=out_specs, check_vma=False)
```

profile of v0, /device:TPU:8, one launch (start us, length us, event | category | flops | bytes accessed | tf_op | source)
XLA Modules:
  0.0 708.7 jit_solution(988738983611834852)
XLA Ops:
  8.9 106.5 %all_gather.18 = bf16[1024,256]{1,0:T(8,128)(2,1)S(1)} all-gather(bf16[16,256]{1,0:T(8,128)(2,1)} %param.16), channel_id=1, replica_groups=mesh['tm'=64,'head'=8] {'tm'}, dimensions={0}, use_global_device_ids=true | all-gather | bytes 532480 | tf_op jit(solution)/shard_map/all_gather | solution.py:104
  115.8 98.0 %all_gather.19 = bf16[1024,256]{1,0:T(8,128)(2,1)S(1)} all-gather(bf16[16,256]{1,0:T(8,128)(2,1)} %param.14), channel_id=1, replica_groups=mesh['tm'=64,'head'=8] {'tm'}, dimensions={0}, use_global_device_ids=true | all-gather | bytes 532480 | tf_op jit(solution)/shard_map/all_gather | solution.py:102
  215.9 16.3 %while.27 = (s32[]{:T(128)}, f32[4,128,64]{1,2,0:T(8,128)S(1)}, f32[2,128,4,64]{1,0,3,2:T(2,128)S(1)}, f32[2,4,128]{2,1,0:T(4,128)}, s32[2,128]{1,0:T(2,128)S(1)...) while((s32[]{:T(128)}, f32[4,128,64]{1,2,0:T(8,128)S(1)}, ...), condition=%wide.region_5.6_spmd.clone, body=%wide.region_3.5_spmd.clone.sunk | while | flops 155747840 | bytes 1896203 | solution.py:61
  220.8 2.6 dynamic_update_slice.6
  229.0 2.6 dynamic_update_slice.6
  234.5 1.3 dynamic-slice
  237.3 121.9 %all-reduce = f32[256]{0:T(256)S(1)} all-reduce(f32[256]{0:T(256)S(1)} %multiply_dynamic-update-slice_fusion), channel_id=2, replica_groups=mesh['tm'=64,'head'=8] {'tm'}, use_global_device_ids=true, to_apply=%add | all-reduce | flops 256 | bytes 2048
  360.0 1.2 reduce-window.11
  361.8 118.6 %all_gather.22 = bf16[1024,256]{1,0:T(8,128)(2,1)S(1)} all-gather(bf16[16,256]{1,0:T(8,128)(2,1)S(1)} %copy-done.3), channel_id=1, replica_groups=mesh['tm'=64,'head'=8] {'tm'}, dimensions={0}, use_global_device_ids=true | all-gather | bytes 532480 | tf_op jit(solution)/shard_map/all_gather | solution.py:103
  480.6 77.0 %while.28 = (s32[]{:T(128)}, f32[4,128,64]{2,1,0:T(8,128)S(1)}, s32[]{:T(128)}, f32[64,4]{1,0:T(8,128)S(1)}, f32[64,4,128,64]{2,3,1,0:T(8,128)}, /*index=5*/s32[]{:T(128)}, s32[]{:T(128)}) while((s32[]{:T(128)}, f32[4,128,64]{2,1,0:T(8,128)S(1)}, s32[]{:T(128)}, f32[64,4]{1,0:T(8,128)S(1)}, f32[64,4,128,64]{2,3,1,0:T(8,128)}, ...), condition=%wide.region_8.9_spmd.clone, body=%wide.region_7.8_spmd.clone.sunk | while | flops 131076 | bytes 917657 | solution.py:141
  484.2 0.9 constant_dynamic-slice_fusion.4
  485.5 0.9 constant_dynamic-slice_fusion.4
  486.7 0.9 constant_dynamic-slice_fusion.4
  487.9 0.9 constant_dynamic-slice_fusion.4
  489.1 0.9 constant_dynamic-slice_fusion.4
  490.3 0.9 constant_dynamic-slice_fusion.4
  491.5 0.9 constant_dynamic-slice_fusion.4
  495.1 0.9 constant_dynamic-slice_fusion.4
  496.3 0.9 constant_dynamic-slice_fusion.4
  497.5 0.9 constant_dynamic-slice_fusion.4
  498.7 0.9 constant_dynamic-slice_fusion.4
  499.9 0.9 constant_dynamic-slice_fusion.4
  501.1 0.9 constant_dynamic-slice_fusion.4
  502.3 0.9 constant_dynamic-slice_fusion.4
  507.1 0.9 constant_dynamic-slice_fusion.4
  508.3 0.9 constant_dynamic-slice_fusion.4
  509.5 0.9 constant_dynamic-slice_fusion.4
  510.7 0.9 constant_dynamic-slice_fusion.4
  511.9 0.9 constant_dynamic-slice_fusion.4
  513.1 0.9 constant_dynamic-slice_fusion.4
  514.3 0.9 constant_dynamic-slice_fusion.4
  517.9 0.9 constant_dynamic-slice_fusion.4
  519.1 0.9 constant_dynamic-slice_fusion.4
  520.3 0.9 constant_dynamic-slice_fusion.4
  521.5 0.9 constant_dynamic-slice_fusion.4
  522.7 0.9 constant_dynamic-slice_fusion.4
  524.0 0.9 constant_dynamic-slice_fusion.4
  525.2 0.9 constant_dynamic-slice_fusion.4
  530.0 0.9 constant_dynamic-slice_fusion.4
  531.2 0.9 constant_dynamic-slice_fusion.4
  532.4 0.9 constant_dynamic-slice_fusion.4
  558.6 1.9 collective-permute-start
  560.5 6.0 collective-permute-start.1
  566.6 96.8 %all_gather.23 = bf16[256,1024]{0,1:T(8,128)(2,1)S(1)} all-gather(bf16[256,16]{0,1:T(8,128)(2,1)S(1)} %copy-done.4), channel_id=1, replica_groups=mesh['tm'=64,'head'=8] {'tm'}, dimensions={1}, use_global_device_ids=true | all-gather | bytes 532480 | tf_op jit(solution)/shard_map/all_gather | solution.py:163
  663.3 3.0 convolution_convert_fusion
  666.4 1.0 copy.47
  667.4 32.9 %reduce-scatter.4.cloned.1.call-done = bf16[128,256]{1,0:T(8,128)(2,1)} async-done(((bf16[1024,256]{1,0:T(8,128)(2,1)}), bf16[128,256]{1,0:T(8,128)(2,1)}) %reduce-scatter.4.cloned.1.call-update) | async-done | bytes 65552
  700.3 1.6 copy.48
  (317 shorter events, 66.2 us)
Async XLA Ops:
  6.5 108.9 %copy-start = (bf16[256,1024]{1,0:T(8,128)(2,1)S(1)}, bf16[256,1024]{1,0:T(8,128)(2,1)}, u32[]{:S(2)}) copy-start(bf16[256,1024]{1,0:T(8,128)(2,1)} %param.13) | copy-start | bytes 1572868
  6.5 355.2 %copy-start.3 = (bf16[16,256]{1,0:T(8,128)(2,1)S(1)}, bf16[16,256]{1,0:T(8,128)(2,1)}, u32[]{:S(2)}) copy-start(bf16[16,256]{1,0:T(8,128)(2,1)} %param.15) | copy-start | bytes 24580
  6.5 473.9 %copy-start.2 = (f32[31,256]{1,0:T(8,128)S(1)}, f32[31,256]{1,0:T(8,128)}, u32[]{:S(2)}) copy-start(f32[31,256]{1,0:T(8,128)} %param.19) | copy-start | bytes 95236
  6.5 474.1 %all-gather.4.cloned.1.call-start = ((), (), s32[]{:S(2)}) async-start(), calls=%async_computation.1 | async-start | bytes 8519680 | tf_op jit(solution)/shard_map/all_gather | solution.py:133
  215.8 342.4 %copy-start.5 = (f32[256]{0:T(256)S(1)}, f32[256]{0:T(256)}, u32[]{:S(2)}) copy-start(f32[256]{0:T(256)} %param.18) | copy-start | bytes 3076
  232.2 0.7 copy-start.1
  232.2 334.4 %copy-start.4 = (bf16[256,16]{0,1:T(8,128)(2,1)S(1)}, bf16[256,16]{0,1:T(8,128)(2,1)}, u32[]{:S(2)}) copy-start(bf16[256,16]{0,1:T(8,128)(2,1)} %param.20) | copy-start | bytes 24580
  232.9 467.4 %reduce-scatter.4.cloned.1.call-start = ((), (), s32[]{:S(2)}) async-start(), calls=%async_computation.2 | async-start | bytes 589824
  558.6 104.7 %collective-permute-start = (bf16[15,256]{1,0:T(8,128)(2,1)S(1)}, bf16[15,256]{1,0:T(8,128)(2,1)S(1)}, u32[]{:S(2)}, u32[]{:S(2)}) collective-permute-start(bf16[15,256]{1,0:T(8,128)(2,1)S(1)} %get-tuple-element.276), channel_id=1, source_target_pairs={{0,8},{8,16},{16,24},{24,32},{32,40},{40,48},{48,56},{56,64},{64,7... | collective-permute-start | bytes 23048 | tf_op jit(solution)/shard_map/ppermute | solution.py:17
  560.5 102.8 %collective-permute-start.1 = (bf16[15,256]{1,0:T(8,128)(2,1)S(1)}, bf16[15,256]{1,0:T(8,128)(2,1)S(1)}, u32[]{:S(2)}, u32[]{:S(2)}) collective-permute-start(bf16[15,256]{1,0:T(8,128)(2,1)S(1)} %get-tuple-element.277), channel_id=1, source_target_pairs={{8,0},{16,8},{24,16},{32,24},{40,32},{48,40},{56,48},{64,56},{72,6... | collective-permute-start | bytes 23048 | tf_op jit(solution)/shard_map/ppermute | solution.py:18
Sparse Core Ops, SparseCore 0:
  233.0 151.7 all-gather.3
  667.5 32.7 reduce-scatter.3
where the time goes:
time: 710 us; the launch traced here: 709 us
  blocking collectives  542 us (76%)
  local copies, waits for them, and re-layouts  85.5 us (12%)
  waiting for transfers between devices  32.9 us (5%)
  other arithmetic  15.8 us (2%)
  between operations  15 us (2%)
  starting transfers between devices  8 us (1%)
    unnamed x1, blocking collectives  122 us
    all_gather x1, blocking collectives, local(): lax.all_gather(z_weight, 'tm', axis=0, tiled=True)  119 us
    all_gather x1, blocking collectives, local(): lax.all_gather(bc_weight, 'tm', axis=0, tiled=True)  107 us
    all_gather x1, blocking collectives, local(): lax.all_gather(x_weight, 'tm', axis=0, tiled=True)  98 us
    all_gather x1, blocking collectives, local(): lax.all_gather(out_weight, 'tm', axis=1, tiled=True)  96.8 us
    dynamic_slice x128, local copies, waits for them, and re-layouts, absorb(): all_summaries[position]  67 us
    unnamed x3, waiting for transfers between devices  32.9 us
  transfers between devices with their start and end apart: 4, of which 1 were waited for; matrix products, arithmetic and copies ran while one was open for 1% of the time, Pallas kernels for 0%

commit v1 on v0

--- a/solution.py
+++ b/solution.py
@@ -1,3 +1,4 @@
+import functools
 import jax
 import jax.numpy as jnp
 from jax import lax
@@ -5,6 +6,19 @@
 
 SPAN = 128
 highest = lax.Precision.HIGHEST
+
+
+def take_the_frame(q_in, shard_axis, axis_no):
+    y2 = jnp.concatenate(
+        lax.all_to_all(
+            jnp.stack(tuple((q_in for _ in range(lax.axis_size(shard_axis))))), shard_axis, 0, 0
+        ),
+        axis=axis_no,
+    )
+    return y2
+
+
+try_all_quarters = functools.partial(take_the_frame, shard_axis="tm", axis_no=0)
 
 
 def extended_2(array, sides, width):
@@ -99,7 +113,7 @@
     frame_count = frames.shape[0]
     state_width = bc_weight.shape[1] // 2
     pieces = (
-        lax.all_gather(x_weight, "tm", axis=0, tiled=True),
+        try_all_quarters(x_weight),
         lax.all_gather(z_weight, "tm", axis=0, tiled=True),
         lax.all_gather(bc_weight, "tm", axis=0, tiled=True),
     )

time: 710 us -> 639 us (0.900)
  blocking collectives: 542 us -> 450 us
  starting transfers between devices: 8 us -> 26.8 us
    all_gather x1 -> x0, blocking collectives: 98 us -> none  [local(): lax.all_gather(x_weight, 'tm', axis=0, tiled=True)]
    all_to_all x0 -> x1, starting transfers between devices: none -> 18.7 us  [take_the_frame(): lax.all_to_all(jnp.stack(tuple((q_in for _ in range(lax.axis_size(shard_a...]
    all_gather x1, blocking collectives: 107 us -> 114 us  [local(): lax.all_gather(bc_weight, 'tm', axis=0, tiled=True)]
  transfers between devices with their start and end apart: 4 -> 5, of which waited for: 1 -> 1; matrix products, arithmetic and copies ran while one was open for 1% -> 2% of each run, Pallas kernels for 0% -> 0%
where the time goes in v1:
time: 639 us; the launch traced here: 637 us
  blocking collectives  450 us (70%)
  local copies, waits for them, and re-layouts  87.1 us (14%)
  waiting for transfers between devices  32.9 us (5%)
  starting transfers between devices  26.8 us (4%)
  other arithmetic  15.8 us (2%)
  between operations  15 us (2%)
  matrix products  6.63 us (1%)
    unnamed x1, blocking collectives  122 us
    all_gather x1, blocking collectives, local(): lax.all_gather(z_weight, 'tm', axis=0, tiled=True)  117 us
    all_gather x1, blocking collectives, local(): lax.all_gather(bc_weight, 'tm', axis=0, tiled=True)  114 us
    all_gather x1, blocking collectives, local(): lax.all_gather(out_weight, 'tm', axis=1, tiled=True)  96.8 us
    dynamic_slice x128, local copies, waits for them, and re-layouts, absorb(): all_summaries[position]  67 us
    unnamed x3, waiting for transfers between devices  32.9 us
    all_to_all x1, starting transfers between devices, take_the_frame(): lax.all_to_all(jnp.stack(tuple((q_in for _ in range(lax.axis_size(shard_a...  18.7 us
  transfers between devices with their start and end apart: 5, of which 1 were waited for; matrix products, arithmetic and copies ran while one was open for 2% of the time, Pallas kernels for 0%

profile of v1, /device:TPU:8, one launch (start us, length us, event | category | flops | bytes accessed | tf_op | source)
XLA Modules:
  0.0 637.3 jit_solution(10012935831148331063)
XLA Ops:
  6.5 1.6 stack.2
  8.1 18.7 %all-to-all-start = ((bf16[64,16,256]{2,1,0:T(8,128)(2,1)}), bf16[64,16,256]{2,1,0:T(8,128)(2,1)S(1)}, u32[]{:S(2)}, u32[]{:S(2)}) async-start(bf16[64,16,256]{2,1,0:T(8,128)(2,1)} %stack.2), calls=%async_computation | async-start | bytes 1048576 | tf_op jit(solution)/shard_map/all_to_all | solution.py:13
  30.6 114.1 %all_gather.15 = bf16[1024,256]{1,0:T(8,128)(2,1)S(1)} all-gather(bf16[16,256]{1,0:T(8,128)(2,1)} %param.16), channel_id=1, replica_groups=mesh['tm'=64,'head'=8] {'tm'}, dimensions={0}, use_global_device_ids=true | all-gather | bytes 532480 | tf_op jit(solution)/shard_map/all_gather | solution.py:118
  145.7 16.4 %while.27 = (s32[]{:T(128)}, f32[4,128,64]{1,2,0:T(8,128)S(1)}, f32[2,128,4,64]{1,0,3,2:T(2,128)S(1)}, f32[2,4,128]{2,1,0:T(4,128)}, s32[2,128]{1,0:T(2,128)S(1)...) while((s32[]{:T(128)}, f32[4,128,64]{1,2,0:T(8,128)S(1)}, ...), condition=%wide.region_5.6_spmd.clone, body=%wide.region_3.5_spmd.clone.sunk | while | flops 155747840 | bytes 1896203 | solution.py:75
  150.7 2.6 dynamic_update_slice.6
  158.9 2.6 dynamic_update_slice.6
  164.4 1.3 dynamic-slice
  167.2 122.4 %all-reduce = f32[256]{0:T(256)S(1)} all-reduce(f32[256]{0:T(256)S(1)} %multiply_dynamic-update-slice_fusion), channel_id=2, replica_groups=mesh['tm'=64,'head'=8] {'tm'}, use_global_device_ids=true, to_apply=%add | all-reduce | flops 256 | bytes 2048
  290.4 1.2 reduce-window.11
  291.9 116.9 %all_gather.18 = bf16[1024,256]{1,0:T(8,128)(2,1)S(1)} all-gather(bf16[16,256]{1,0:T(8,128)(2,1)S(1)} %copy-done.3), channel_id=1, replica_groups=mesh['tm'=64,'head'=8] {'tm'}, dimensions={0}, use_global_device_ids=true | all-gather | bytes 532480 | tf_op jit(solution)/shard_map/all_gather | solution.py:117
  409.2 77.0 %while.28 = (s32[]{:T(128)}, f32[4,128,64]{2,1,0:T(8,128)S(1)}, s32[]{:T(128)}, f32[64,4]{1,0:T(8,128)S(1)}, f32[64,4,128,64]{2,3,1,0:T(8,128)}, /*index=5*/s32[]{:T(128)}, s32[]{:T(128)}) while((s32[]{:T(128)}, f32[4,128,64]{2,1,0:T(8,128)S(1)}, s32[]{:T(128)}, f32[64,4]{1,0:T(8,128)S(1)}, f32[64,4,128,64]{2,3,1,0:T(8,128)}, ...), condition=%wide.region_8.9_spmd.clone, body=%wide.region_7.8_spmd.clone.sunk | while | flops 131076 | bytes 917657 | solution.py:155
  409.3 0.9 constant_dynamic-slice_fusion.4
  410.5 0.9 constant_dynamic-slice_fusion.4
  411.7 0.9 constant_dynamic-slice_fusion.4
  412.9 0.9 constant_dynamic-slice_fusion.4
  417.7 0.9 constant_dynamic-slice_fusion.4
  418.9 0.9 constant_dynamic-slice_fusion.4
  420.1 0.9 constant_dynamic-slice_fusion.4
  421.3 0.9 constant_dynamic-slice_fusion.4
  422.5 0.9 constant_dynamic-slice_fusion.4
  423.7 0.9 constant_dynamic-slice_fusion.4
  424.9 0.9 constant_dynamic-slice_fusion.4
  428.5 0.9 constant_dynamic-slice_fusion.4
  429.7 0.9 constant_dynamic-slice_fusion.4
  430.9 0.9 constant_dynamic-slice_fusion.4
  432.1 0.9 constant_dynamic-slice_fusion.4
  433.3 0.9 constant_dynamic-slice_fusion.4
  434.5 0.9 constant_dynamic-slice_fusion.4
  435.7 0.9 constant_dynamic-slice_fusion.4
  440.5 0.9 constant_dynamic-slice_fusion.4
  441.7 0.9 constant_dynamic-slice_fusion.4
  442.9 0.9 constant_dynamic-slice_fusion.4
  444.1 0.9 constant_dynamic-slice_fusion.4
  445.4 0.9 constant_dynamic-slice_fusion.4
  446.6 0.9 constant_dynamic-slice_fusion.4
  447.8 0.9 constant_dynamic-slice_fusion.4
  451.4 0.9 constant_dynamic-slice_fusion.4
  452.6 0.9 constant_dynamic-slice_fusion.4
  453.8 0.9 constant_dynamic-slice_fusion.4
  455.0 0.9 constant_dynamic-slice_fusion.4
  456.2 0.9 constant_dynamic-slice_fusion.4
  487.2 1.9 collective-permute-start
  489.1 6.0 collective-permute-start.1
  495.2 96.8 %all_gather.19 = bf16[256,1024]{0,1:T(8,128)(2,1)S(1)} all-gather(bf16[256,16]{0,1:T(8,128)(2,1)S(1)} %copy-done.4), channel_id=1, replica_groups=mesh['tm'=64,'head'=8] {'tm'}, dimensions={1}, use_global_device_ids=true | all-gather | bytes 532480 | tf_op jit(solution)/shard_map/all_gather | solution.py:177
  592.0 3.0 convolution_convert_fusion
  595.0 1.0 copy.47
  596.0 32.9 %reduce-scatter.4.cloned.1.call-done = bf16[128,256]{1,0:T(8,128)(2,1)} async-done(((bf16[1024,256]{1,0:T(8,128)(2,1)}), bf16[128,256]{1,0:T(8,128)(2,1)}) %reduce-scatter.4.cloned.1.call-update) | async-done | bytes 65552
  628.9 1.6 copy.48
  (319 shorter events, 67.1 us)
Async XLA Ops:
  6.5 138.2 %copy-start = (bf16[256,1024]{1,0:T(8,128)(2,1)S(1)}, bf16[256,1024]{1,0:T(8,128)(2,1)}, u32[]{:S(2)}) copy-start(bf16[256,1024]{1,0:T(8,128)(2,1)} %param.13) | copy-start | bytes 1572868
  6.5 285.3 %copy-start.3 = (bf16[16,256]{1,0:T(8,128)(2,1)S(1)}, bf16[16,256]{1,0:T(8,128)(2,1)}, u32[]{:S(2)}) copy-start(bf16[16,256]{1,0:T(8,128)(2,1)} %param.15) | copy-start | bytes 24580
  6.5 402.3 %copy-start.2 = (f32[31,256]{1,0:T(8,128)S(1)}, f32[31,256]{1,0:T(8,128)}, u32[]{:S(2)}) copy-start(f32[31,256]{1,0:T(8,128)} %param.19) | copy-start | bytes 95236
  8.1 136.9 %all-to-all-start = ((bf16[64,16,256]{2,1,0:T(8,128)(2,1)}), bf16[64,16,256]{2,1,0:T(8,128)(2,1)S(1)}, u32[]{:S(2)}, u32[]{:S(2)}) async-start(bf16[64,16,256]{2,1,0:T(8,128)(2,1)} %stack.2), calls=%async_computation | async-start | bytes 1048576 | tf_op jit(solution)/shard_map/all_to_all | solution.py:13
  26.9 382.4 %all-gather.4.cloned.1.call-start = ((), (), s32[]{:S(2)}) async-start(), calls=%async_computation.2 | async-start | bytes 8519680 | tf_op jit(solution)/shard_map/all_gather | solution.py:147
  145.7 341.2 %copy-start.5 = (f32[256]{0:T(256)S(1)}, f32[256]{0:T(256)}, u32[]{:S(2)}) copy-start(f32[256]{0:T(256)} %param.18) | copy-start | bytes 3076
  162.1 0.7 copy-start.1
  162.1 333.1 %copy-start.4 = (bf16[256,16]{0,1:T(8,128)(2,1)S(1)}, bf16[256,16]{0,1:T(8,128)(2,1)}, u32[]{:S(2)}) copy-start(bf16[256,16]{0,1:T(8,128)(2,1)} %param.20) | copy-start | bytes 24580
  162.7 466.1 %reduce-scatter.4.cloned.1.call-start = ((), (), s32[]{:S(2)}) async-start(), calls=%async_computation.3 | async-start | bytes 589824
  487.2 104.7 %collective-permute-start = (bf16[15,256]{1,0:T(8,128)(2,1)S(1)}, bf16[15,256]{1,0:T(8,128)(2,1)S(1)}, u32[]{:S(2)}, u32[]{:S(2)}) collective-permute-start(bf16[15,256]{1,0:T(8,128)(2,1)S(1)} %get-tuple-element.276), channel_id=1, source_target_pairs={{0,8},{8,16},{16,24},{24,32},{32,40},{40,48},{48,56},{56,64},{64,7... | collective-permute-start | bytes 23048 | tf_op jit(solution)/shard_map/ppermute | solution.py:31
  489.1 102.8 %collective-permute-start.1 = (bf16[15,256]{1,0:T(8,128)(2,1)S(1)}, bf16[15,256]{1,0:T(8,128)(2,1)S(1)}, u32[]{:S(2)}, u32[]{:S(2)}) collective-permute-start(bf16[15,256]{1,0:T(8,128)(2,1)S(1)} %get-tuple-element.277), channel_id=1, source_target_pairs={{8,0},{16,8},{24,16},{32,24},{40,32},{48,40},{56,48},{64,56},{72,6... | collective-permute-start | bytes 23048 | tf_op jit(solution)/shard_map/ppermute | solution.py:32
Sparse Core Ops, SparseCore 0:
  162.9 154.1 all-gather.3
  596.1 32.7 reduce-scatter.3
